TPU v7x, 32 devices: a whole 2x2x4 slice. The times are simulated.
32 devices in a mesh: group: 2 (over y), seq: 4 (over z), tensor: 4 (over x, core).
Axes of the slice: x: 2, y: 2, z: 4, core: 2. Of those that a mesh axis runs over, the one named last changes fastest.
Arguments:
- spans: bfloat16 [1024, 3072], P(('group', 'seq')), parts along dimension 0, may hold values from -6 to 6
- w_in: bfloat16 [3072, 1024], P(None, 'tensor'), may hold values from -0.109375 to 0.109375
- band_weights: bfloat16 [4096, 128], P(('group', 'seq')), parts along dimension 0
- offsets: int32 [32], P(('group', 'seq')), parts along dimension 0, may hold values from 0 to 384, as said below
- w_up: bfloat16 [1024, 4096], P(None, 'tensor'), may hold values from -0.1875 to 0.1875
- d_up: bfloat16 [4096, 4096], P(('group', 'seq'), 'tensor'), parts along dimension 0, may hold values from -3 to 3
Outputs:
- up_proj: bfloat16 [4096, 4096], P(('group', 'seq'), 'tensor'), parts along dimension 0
- d_spans: bfloat16 [1024, 3072], P(('group', 'seq'), 'tensor'), parts along dimension 0
There are 2 independent parts, one for each index of `group`. A program takes and returns all parts, laid end to end along the dimension named above; an argument that names none is the same for every part. Nothing has to cross between parts.
Inputs may be any that keep to these rules, and one draw needn't show every extreme that they name: offsets[b] differs from b * 384 // 15 by at most 128, and both differences -128 and +128 occur in every draw; offsets[0] = 0 and offsets[15] = 384. Hence the bands of the bytes of seq index i lie within the span rows of seq indices i - 3 to i + 3.
All inputs are finite; a program needn't handle non-finite values.
Results may differ from a plain program's by a relative error of at most 0.0058.
Values may be sent and summed in bfloat16 or wider, within the bound.
No kernel may reach another device: no remote copies, remote signals or barrier semaphores. Data moves between devices by JAX's collectives and lax.ppermute only.
A program may use at most 64 MiB of HBM per device.

v0:
```python
import jax
import jax.numpy as jnp
from jax import lax
from jax.sharding import PartitionSpec as P


def band_matrix(band_weights, offsets, anchor, length):
    blocks = offsets.shape[0]
    breadth = band_weights.shape[1]
    band_cube = band_weights.reshape(blocks, -1, breadth)
    relative = anchor + jnp.arange(length, dtype=jnp.int32)[None, :] - offsets[:, None]
    picker = (relative[:, None, :] == jnp.arange(breadth, dtype=jnp.int32)[None, :, None]).astype(
        jnp.bfloat16
    )
    spread = jnp.einsum("bij,bjr->bir", band_cube, picker, preferred_element_type=jnp.float32)
    return spread.astype(jnp.bfloat16).reshape(-1, length)


def touches(offsets, breadth, anchor, length):
    return jnp.any((offsets < anchor + length) & (offsets + breadth > anchor))


def body(spans, w_in, band_weights, offsets, w_up, d_up):
    breadth = band_weights.shape[1]
    reduced = jnp.dot(spans, w_in, preferred_element_type=jnp.float32).astype(jnp.bfloat16)
    feature_count = reduced.shape[1]
    span_rows = reduced.shape[0]
    initial = jnp.zeros((band_weights.shape[0], feature_count), jnp.float32)
    shard_rows = lax.all_gather(reduced, "seq", axis=0, tiled=True)
    anchor = jnp.int32(0)
    length = shard_rows.shape[0]

    def accumulate(current):
        spread = band_matrix(band_weights, offsets, anchor, length)
        return jnp.dot(spread, shard_rows, preferred_element_type=jnp.float32)

    def unchanged(current):
        return current

    upsampled = lax.cond(
        touches(offsets, breadth, anchor, length), accumulate, unchanged, initial
    ).astype(jnp.bfloat16)
    gathered = lax.all_gather(upsampled, "tensor", axis=1, tiled=True)
    up_proj = jnp.dot(gathered, w_up, preferred_element_type=jnp.float32).astype(jnp.bfloat16)
    grad_cols = lax.psum_scatter(
        lax.dot_general(w_up, d_up, (((1,), (1,)), ((), ())), preferred_element_type=jnp.float32),
        "tensor",
        scatter_dimension=0,
        tiled=True,
    ).astype(jnp.bfloat16)

    def compute(operand):
        spread = band_matrix(band_weights, offsets, 0, span_rows * lax.axis_size("seq"))
        return lax.dot_general(
            spread, grad_cols, (((0,), (1,)), ((), ())), preferred_element_type=jnp.float32
        )

    def nothing(operand):
        return jnp.zeros((span_rows * lax.axis_size("seq"), feature_count), jnp.float32)

    every_row = lax.psum(
        lax.cond(
            touches(offsets, breadth, 0, span_rows * lax.axis_size("seq")), compute, nothing, 0
        ),
        "seq",
    )
    d_reduced = lax.dynamic_slice_in_dim(every_row, lax.axis_index("seq") * span_rows, span_rows, 0)
    d_reduced = d_reduced.astype(jnp.bfloat16)
    feature_parts = lax.dot_general(
        d_reduced, w_in, (((1,), (1,)), ((), ())), preferred_element_type=jnp.float32
    )
    d_spans = lax.psum_scatter(feature_parts, "tensor", scatter_dimension=1, tiled=True).astype(
        jnp.bfloat16
    )
    return (up_proj, d_spans)


def solution(mesh):
    placed = (
        P(("group", "seq"), None),
        P(None, "tensor"),
        P(("group", "seq"), None),
        P(("group", "seq")),
        P(None, "tensor"),
        P(("group", "seq"), "tensor"),
    )
    return jax.shard_map(
        body,
        mesh=mesh,
        in_specs=placed,
        out_specs=(P(("group", "seq"), "tensor"), P(("group", "seq"), "tensor")),
        check_vma=False,
    )
```

profile of v0, /device:TPU:0, one launch (start us, length us, event | category | flops | bytes accessed | tf_op | source)
XLA Modules:
  0.0 116.6 jit_solution(14578127177563211295)
XLA Ops:
  7.2 0.0 copy-start
  7.2 0.0 reduce-scatter.3.cloned.1.call-start
  7.2 1.5 %copy-done = bf16[1024,1024]{1,0:T(8,128)(2,1)S(1)} copy-done((bf16[1024,1024]{1,0:T(8,128)(2,1)S(1)}, bf16[1024,1024]{1,0:T(8,128)(2,1)}, u32[]{:S(2)}) %copy-start) | copy-done | bytes 2097176
  8.8 3.9 %fusion.6 = f32[1024,512]{1,0:T(8,128)} fusion(bf16[1024,1024]{1,0:T(8,128)(2,1)S(1)} %copy-done, bf16[512,1024]{1,0:T(8,128)(2,1)} %param.15), kind=kOutput, calls=%fused_computation.16 | convolution fusion | flops 1073741824 | bytes 5242880 | tf_op jit(solution)/shard_map/dot_general | solution.py:46
  12.6 0.0 copy-start.4
  12.6 0.0 copy-start.2
  12.6 0.0 copy-start.3
  12.6 0.0 reduce-scatter.3.cloned.1.call-update
  12.7 0.0 all-gather.2.cloned.1.call-start
  12.7 0.6 copy-done.4
  13.3 0.6 and_reduce_fusion
  14.6 0.0 copy-done.2
  14.6 1.8 %convolution_convert_fusion.3 = bf16[128,256]{1,0:T(8,128)(2,1)S(1)} fusion(bf16[128,3072]{1,0:T(8,128)(2,1)S(1)} %copy-done.2, bf16[3072,256]{1,0:T(8,128)(2,1)} %param.11), kind=kOutput, calls=%fused_computation.9 | convolution fusion | flops 201359360 | bytes 2424832 | tf_op jit(solution)/shard_map/dot_general | solution.py:25
  16.4 15.6 %all_gather.6 = bf16[512,256]{1,0:T(8,128)(2,1)S(1)} all-gather(bf16[128,256]{1,0:T(8,128)(2,1)S(1)} %convolution_convert_fusion.3), channel_id=1, replica_groups=mesh['group'=2,'seq'=4,'tensor'=4] {'seq'}, dimensions={0}, use_global_device_ids=true | all-gather | bytes 327680 | tf_op jit(solution)/shard_map/all_gather | solution.py:29
  32.0 0.0 copy-done.3
  32.0 0.7 conditional.2
  32.0 0.1 iota_subtract_fusion
  32.1 0.3 convolution_convert_fusion
  32.4 0.3 fusion.4
  32.7 0.0 copy-start.1
  32.7 0.7 copy-done.1
  33.4 0.0 all-gather.2.cloned.1.call-update
  33.5 0.0 reduce-scatter.5.cloned.1.call-start
  33.5 13.4 %reduce-scatter.3.cloned.1.call-done = f32[256,512]{1,0:T(8,128)} async-done(((f32[1024,512]{1,0:T(8,128)}), f32[256,512]{1,0:T(8,128)}) %reduce-scatter.3.cloned.1.call-update) | async-done | bytes 524304 | tf_op jit(solution)/shard_map/reduce_scatter | solution.py:45
  46.9 1.1 convert_element_type.40
  48.0 0.8 conditional.3
  48.0 0.1 iota_subtract_fusion.1
  48.1 0.3 convolution_convert_fusion.1
  48.5 0.3 fusion.5
  48.8 30.5 %all-reduce.1 = bf16[512,256]{1,0:T(8,128)(2,1)S(1)} all-reduce(f32[512,256]{1,0:T(8,128)S(1)} %get-tuple-element.27), channel_id=1, replica_groups=mesh['group'=2,'seq'=4,'tensor'=4] {'seq'}, use_global_device_ids=true, to_apply=%region_6.0 | all-reduce | flops 131072 | bytes 786432 | tf_op jit(solution)/shard_map/psum | solution.py:61
  79.3 3.2 %fusion.2 = f32[128,3072]{1,0:T(8,128)} fusion(bf16[3072,256]{1,0:T(8,128)(2,1)} %param.11, bf16[512,256]{1,0:T(8,128)(2,1)S(1)} %all-reduce.1, s32[]{:T(128)S(6)} %select_n.3), kind=kOutput, calls=%fused_computation.11 | convolution fusion | flops 201326592 | bytes 3211268 | tf_op jit(solution)/shard_map/dot_general | solution.py:69
  82.5 0.0 reduce-scatter.5.cloned.1.call-update
  82.5 0.0 all-gather.2.cloned.1.call-done
  82.5 3.4 %convolution_convert_fusion.2 = bf16[512,1024]{1,0:T(8,128)(2,1)} fusion(bf16[512,1024]{1,0:T(8,128)(2,1)} %all-gather.2.cloned.1.call-done, bf16[1024,1024]{1,0:T(8,128)(2,1)S(1)} %copy-done), kind=kOutput, calls=%fused_computation.8 | convolution fusion | flops 1074266112 | bytes 4194304 | tf_op jit(solution)/shard_map/dot_general | solution.py:44
  86.0 22.4 %reduce-scatter.5.cloned.1.call-done = f32[128,768]{1,0:T(8,128)} async-done(((f32[128,3072]{1,0:T(8,128)}), f32[128,768]{1,0:T(8,128)}) %reduce-scatter.5.cloned.1.call-update) | async-done | bytes 393232 | tf_op jit(solution)/shard_map/reduce_scatter | solution.py:72
  108.4 1.7 %convert_element_type.42 = bf16[128,768]{1,0:T(8,128)(2,1)} convert(f32[128,768]{1,0:T(8,128)} %reduce-scatter.5.cloned.1.call-done) | non-fusion elementwise | flops 98304 | bytes 589824 | tf_op jit(solution)/shard_map/convert_element_type | solution.py:72
Async XLA Ops:
  7.2 1.6 %copy-start = (bf16[1024,1024]{1,0:T(8,128)(2,1)S(1)}, bf16[1024,1024]{1,0:T(8,128)(2,1)}, u32[]{:S(2)}) copy-start(bf16[1024,1024]{1,0:T(8,128)(2,1)} %param.14) | copy-start | bytes 6291460
  7.2 39.8 %reduce-scatter.3.cloned.1.call-start = ((), (), s32[]{:S(2)}) async-start(), calls=%async_computation.3 | async-start | bytes 2621440 | tf_op jit(solution)/shard_map/reduce_scatter | solution.py:45
  12.6 0.7 copy-start.4
  12.6 1.9 %copy-start.2 = (bf16[128,3072]{1,0:T(8,128)(2,1)S(1)}, bf16[128,3072]{1,0:T(8,128)(2,1)}, u32[]{:S(2)}) copy-start(bf16[128,3072]{1,0:T(8,128)(2,1)} %param.10) | copy-start | bytes 2359300
  12.6 19.4 %copy-start.3 = (bf16[512,128]{1,0:T(8,128)(2,1)S(1)}, bf16[512,128]{1,0:T(8,128)(2,1)}, u32[]{:S(2)}) copy-start(bf16[512,128]{1,0:T(8,128)(2,1)} %param.12) | copy-start | bytes 393220
  12.7 69.9 %all-gather.2.cloned.1.call-start = ((), (), s32[]{:S(2)}) async-start(), calls=%async_computation.2 | async-start | bytes 1310720 | tf_op jit(solution)/shard_map/all_gather | solution.py:43
  32.7 0.7 copy-start.1
  33.5 74.9 %reduce-scatter.5.cloned.1.call-start = ((), (), s32[]{:S(2)}) async-start(), calls=%async_computation.4 | async-start | bytes 1966080 | tf_op jit(solution)/shard_map/reduce_scatter | solution.py:72
Sparse Core Ops, SparseCore 0:
  12.8 34.1 reduce-scatter.2
  49.1 16.8 all-gather.1
  82.6 25.7 reduce-scatter.4
where the time goes:
time: 117 us
  blocking collectives  46.1 us (39%)
  waiting for transfers between devices  35.9 us (31%)
  between operations  14.5 us (12%)
  matrix products  13.6 us (12%)
  other arithmetic  3.54 us (3%)
  local copies, waits for them, and re-layouts  2.83 us (2%)
    psum x1, blocking collectives, body(): lax.psum(lax.cond(touches(offsets, breadth, 0, span_rows * lax.axis_size(...  30.5 us
    reduce_scatter x1, waiting for transfers between devices, body(): lax.psum_scatter(feature_parts, 'tensor', scatter_dimension=1, tiled=True)  22.4 us
    all_gather x1, blocking collectives, body(): shard_rows = lax.all_gather(reduced, 'seq', axis=0, tiled=True)  15.6 us
    reduce_scatter x1, waiting for transfers between devices, body(): lax.psum_scatter(lax.dot_general(w_up, d_up, (((1,), (1,)), ((), ())), pr...  13.4 us
    dot_general x1, matrix products, body(): lax.dot_general(w_up, d_up, (((1,), (1,)), ((), ())), preferred_element_t...  3.86 us
    dot_general x1, matrix products, body(): jnp.dot(gathered, w_up, preferred_element_type=jnp.float32)  3.45 us
    dot_general x1, matrix products, body(): lax.dot_general(d_reduced, w_in, (((1,), (1,)), ((), ())), preferred_elem...  3.22 us
    unnamed x10, local copies, waits for them, and re-layouts  2.83 us
  transfers between devices with their start and end apart: 3, of which 2 were waited for; matrix products, arithmetic and copies ran while one was open for 10% of the time, Pallas kernels for 0%

commit v1 on v0

--- a/solution.py
+++ b/solution.py
@@ -26,7 +26,12 @@
     feature_count = reduced.shape[1]
     span_rows = reduced.shape[0]
     initial = jnp.zeros((band_weights.shape[0], feature_count), jnp.float32)
-    shard_rows = lax.all_gather(reduced, "seq", axis=0, tiled=True)
+    ring = [reduced]
+    for hop in range(3):
+        ring.append(lax.ppermute(ring[-1], "seq", [(dev, (dev + 1) % 4) for dev in range(4)]))
+    shard_rows = jnp.roll(
+        jnp.concatenate(ring[::-1], axis=0), (lax.axis_index("seq") + 1) * ring[0].shape[0], axis=0
+    )
     anchor = jnp.int32(0)
     length = shard_rows.shape[0]
 

time: 117 us -> 117 us (level)
  blocking collectives: 46.1 us -> 30.3 us
  waiting for transfers between devices: 35.9 us -> 48 us
  starting transfers between devices: 0.12 us -> 3.2 us
    all_gather x1 -> x0, blocking collectives: 15.6 us -> none  [body(): shard_rows = lax.all_gather(reduced, 'seq', axis=0, tiled=True)]
    ppermute x0 -> x3, waiting for transfers between devices: none -> 15.1 us  [body(): lax.ppermute(ring[-1], 'seq', [(dev, (dev + 1) % 4) for dev in range(4)])]
    reduce_scatter x1, waiting for transfers between devices: 13.4 us -> 10.2 us  [body(): lax.psum_scatter(lax.dot_general(w_up, d_up, (((1,), (1,)), ((), ())), pr...]
    ppermute x0 -> x3, starting transfers between devices: none -> 3.08 us  [body(): lax.ppermute(ring[-1], 'seq', [(dev, (dev + 1) % 4) for dev in range(4)])]
    unnamed x10 -> x17, local copies, waits for them, and re-layouts: 2.83 us -> 3.34 us
  transfers between devices with their start and end apart: 3 -> 6, of which waited for: 2 -> 5; matrix products, arithmetic and copies ran while one was open for 10% -> 10% of each run, Pallas kernels for 0% -> 0%
where the time goes in v1:
time: 117 us
  waiting for transfers between devices  48 us (41%)
  blocking collectives  30.3 us (26%)
  between operations  14.5 us (12%)
  matrix products  13.6 us (12%)
  other arithmetic  3.54 us (3%)
  local copies, waits for them, and re-layouts  3.35 us (3%)
  starting transfers between devices  3.2 us (3%)
    psum x1, blocking collectives, body(): lax.psum(lax.cond(touches(offsets, breadth, 0, span_rows * lax.axis_size(...  30.3 us
    reduce_scatter x1, waiting for transfers between devices, body(): lax.psum_scatter(feature_parts, 'tensor', scatter_dimension=1, tiled=True)  22.6 us
    ppermute x3, waiting for transfers between devices, body(): lax.ppermute(ring[-1], 'seq', [(dev, (dev + 1) % 4) for dev in range(4)])  15.1 us
    reduce_scatter x1, waiting for transfers between devices, body(): lax.psum_scatter(lax.dot_general(w_up, d_up, (((1,), (1,)), ((), ())), pr...  10.2 us
    dot_general x1, matrix products, body(): lax.dot_general(w_up, d_up, (((1,), (1,)), ((), ())), preferred_element_t...  3.85 us
    dot_general x1, matrix products, body(): jnp.dot(gathered, w_up, preferred_element_type=jnp.float32)  3.45 us
    unnamed x17, local copies, waits for them, and re-layouts  3.34 us
    dot_general x1, matrix products, body(): lax.dot_general(d_reduced, w_in, (((1,), (1,)), ((), ())), preferred_elem...  3.21 us
  transfers between devices with their start and end apart: 6, of which 5 were waited for; matrix products, arithmetic and copies ran while one was open for 10% of the time, Pallas kernels for 0%

profile of v1, /device:TPU:0, one launch (start us, length us, event | category | flops | bytes accessed | tf_op | source)
XLA Modules:
  0.0 116.6 jit_solution(1669245863912609860)
XLA Ops:
  7.2 0.0 copy-start
  7.2 0.0 reduce-scatter.3.cloned.1.call-start
  7.2 1.5 %copy-done = bf16[1024,1024]{1,0:T(8,128)(2,1)S(1)} copy-done((bf16[1024,1024]{1,0:T(8,128)(2,1)S(1)}, bf16[1024,1024]{1,0:T(8,128)(2,1)}, u32[]{:S(2)}) %copy-start) | copy-done | bytes 2097176
  8.8 3.8 %fusion.8 = f32[1024,512]{1,0:T(8,128)} fusion(bf16[1024,1024]{1,0:T(8,128)(2,1)S(1)} %copy-done, bf16[512,1024]{1,0:T(8,128)(2,1)} %param.15), kind=kOutput, calls=%fused_computation.26 | convolution fusion | flops 1073741824 | bytes 5242880 | tf_op jit(solution)/shard_map/dot_general | solution.py:51
  12.6 0.0 copy-start.2
  12.6 0.0 copy-start.4
  12.6 0.0 reduce-scatter.3.cloned.1.call-update
  12.6 0.0 copy-start.3
  12.7 0.0 all-gather.2.cloned.1.call-start
  12.7 1.0 copy-done.2
  13.7 1.8 %convolution_convert_fusion.3 = bf16[128,256]{1,0:T(8,128)(2,1)S(1)} fusion(bf16[128,3072]{1,0:T(8,128)(2,1)S(1)} %copy-done.2, bf16[3072,256]{1,0:T(8,128)(2,1)} %param.11), kind=kOutput, calls=%fused_computation.12 | convolution fusion | flops 201359360 | bytes 2424832 | tf_op jit(solution)/shard_map/dot_general | solution.py:25
  15.5 3.1 %collective-permute-start = (bf16[128,256]{1,0:T(8,128)(2,1)S(1)}, bf16[128,256]{1,0:T(8,128)(2,1)S(1)}, u32[]{:S(2)}, u32[]{:S(2)}) collective-permute-start(bf16[128,256]{1,0:T(8,128)(2,1)S(1)} %convolution_convert_fusion.3), channel_id=1, source_target_pairs={{0,4},{4,8},{8,12},{12,0},{1,5},{5,9},{9,13},{13,1},{2,6},{6,10},{... | collective-permute-start | bytes 196616 | tf_op jit(solution)/shard_map/ppermute | solution.py:31
  18.6 4.3 %collective-permute-done = bf16[128,256]{1,0:T(8,128)(2,1)S(1)} collective-permute-done((bf16[128,256]{1,0:T(8,128)(2,1)S(1)}, bf16[128,256]{1,0:T(8,128)(2,1)S(1)}, u32[]{:S(2)}, u32[]{:S(2)}) %collective-permute-start) | collective-permute-done | bytes 65568 | tf_op jit(solution)/shard_map/ppermute | solution.py:31
  22.9 0.0 collective-permute-start.1
  22.9 6.1 %collective-permute-done.1 = bf16[128,256]{1,0:T(8,128)(2,1)S(1)} collective-permute-done((bf16[128,256]{1,0:T(8,128)(2,1)S(1)}, bf16[128,256]{1,0:T(8,128)(2,1)S(1)}, u32[]{:S(2)}, u32[]{:S(2)}) %collective-permute-start.1) | collective-permute-done | bytes 65568 | tf_op jit(solution)/shard_map/ppermute | solution.py:31
  29.0 0.0 collective-permute-start.2
  29.0 0.0 copy-done.4
  29.0 0.6 and_reduce_fusion
  30.2 4.8 %collective-permute-done.2 = bf16[128,256]{1,0:T(8,128)(2,1)S(1)} collective-permute-done((bf16[128,256]{1,0:T(8,128)(2,1)S(1)}, bf16[128,256]{1,0:T(8,128)(2,1)S(1)}, u32[]{:S(2)}, u32[]{:S(2)}) %collective-permute-start.2) | collective-permute-done | bytes 65568 | tf_op jit(solution)/shard_map/ppermute | solution.py:31
  35.1 0.0 copy-done.3
  35.1 0.8 conditional.2
  35.2 0.1 iota_subtract_fusion.1
  35.2 0.3 convolution_convert_fusion.1
  35.6 0.3 fusion.2
  35.9 0.0 copy-start.1
  35.9 0.7 copy-done.1
  36.6 0.0 all-gather.2.cloned.1.call-update
  36.6 0.0 reduce-scatter.5.cloned.1.call-start
  36.7 10.2 %reduce-scatter.3.cloned.1.call-done = f32[256,512]{1,0:T(8,128)} async-done(((f32[1024,512]{1,0:T(8,128)}), f32[256,512]{1,0:T(8,128)}) %reduce-scatter.3.cloned.1.call-update) | async-done | bytes 524304 | tf_op jit(solution)/shard_map/reduce_scatter | solution.py:50
  46.9 1.1 convert_element_type.40
  48.0 0.8 conditional.3
  48.0 0.1 iota_subtract_fusion
  48.1 0.3 convolution_convert_fusion
  48.4 0.3 fusion.7
  48.8 30.3 %all-reduce.1 = bf16[512,256]{1,0:T(8,128)(2,1)S(1)} all-reduce(f32[512,256]{1,0:T(8,128)S(1)} %get-tuple-element.52), channel_id=1, replica_groups=mesh['group'=2,'seq'=4,'tensor'=4] {'seq'}, use_global_device_ids=true, to_apply=%region_6.7 | all-reduce | flops 131072 | bytes 786432 | tf_op jit(solution)/shard_map/psum | solution.py:66
  79.1 3.2 %fusion.5 = f32[128,3072]{1,0:T(8,128)} fusion(bf16[3072,256]{1,0:T(8,128)(2,1)} %param.11, bf16[512,256]{1,0:T(8,128)(2,1)S(1)} %all-reduce.1, s32[]{:T(128)S(6)} %select_n.18), kind=kOutput, calls=%fused_computation.14 | convolution fusion | flops 201326592 | bytes 3211268 | tf_op jit(solution)/shard_map/dot_general | solution.py:74
  82.3 0.0 reduce-scatter.5.cloned.1.call-update
  82.3 0.0 all-gather.2.cloned.1.call-done
  82.3 3.4 %convolution_convert_fusion.2 = bf16[512,1024]{1,0:T(8,128)(2,1)} fusion(bf16[512,1024]{1,0:T(8,128)(2,1)} %all-gather.2.cloned.1.call-done, bf16[1024,1024]{1,0:T(8,128)(2,1)S(1)} %copy-done), kind=kOutput, calls=%fused_computation.11 | convolution fusion | flops 1074266112 | bytes 4194304 | tf_op jit(solution)/shard_map/dot_general | solution.py:49
  85.8 22.6 %reduce-scatter.5.cloned.1.call-done = f32[128,768]{1,0:T(8,128)} async-done(((f32[128,3072]{1,0:T(8,128)}), f32[128,768]{1,0:T(8,128)}) %reduce-scatter.5.cloned.1.call-update) | async-done | bytes 393232 | tf_op jit(solution)/shard_map/reduce_scatter | solution.py:77
  108.4 1.7 %convert_element_type.42 = bf16[128,768]{1,0:T(8,128)(2,1)} convert(f32[128,768]{1,0:T(8,128)} %reduce-scatter.5.cloned.1.call-done) | non-fusion elementwise | flops 98304 | bytes 589824 | tf_op jit(solution)/shard_map/convert_element_type | solution.py:77
  (8 shorter events, 0.1 us)
Async XLA Ops:
  7.2 1.6 %copy-start = (bf16[1024,1024]{1,0:T(8,128)(2,1)S(1)}, bf16[1024,1024]{1,0:T(8,128)(2,1)}, u32[]{:S(2)}) copy-start(bf16[1024,1024]{1,0:T(8,128)(2,1)} %param.14) | copy-start | bytes 6291460
  7.2 39.8 %reduce-scatter.3.cloned.1.call-start = ((), (), s32[]{:S(2)}) async-start(), calls=%async_computation.3 | async-start | bytes 2621440 | tf_op jit(solution)/shard_map/reduce_scatter | solution.py:50
  12.6 1.1 copy-start.2
  12.6 16.3 %copy-start.4 = (s32[4]{0:T(128)S(1)}, s32[4]{0:T(128)}, u32[]{:S(2)}) copy-start(s32[4]{0:T(128)} %param.13) | copy-start | bytes 52
  12.6 22.5 %copy-start.3 = (bf16[512,128]{1,0:T(8,128)(2,1)S(1)}, bf16[512,128]{1,0:T(8,128)(2,1)}, u32[]{:S(2)}) copy-start(bf16[512,128]{1,0:T(8,128)(2,1)} %param.12) | copy-start | bytes 393220
  12.7 69.7 %all-gather.2.cloned.1.call-start = ((), (), s32[]{:S(2)}) async-start(), calls=%async_computation.2 | async-start | bytes 1310720 | tf_op jit(solution)/shard_map/all_gather | solution.py:48
  15.5 7.3 %collective-permute-start = (bf16[128,256]{1,0:T(8,128)(2,1)S(1)}, bf16[128,256]{1,0:T(8,128)(2,1)S(1)}, u32[]{:S(2)}, u32[]{:S(2)}) collective-permute-start(bf16[128,256]{1,0:T(8,128)(2,1)S(1)} %convolution_convert_fusion.3), channel_id=1, source_target_pairs={{0,4},{4,8},{8,12},{12,0},{1,5},{5,9},{9,13},{13,1},{2,6},{6,10},{... | collective-permute-start | bytes 196616 | tf_op jit(solution)/shard_map/ppermute | solution.py:31
  22.9 6.1 %collective-permute-start.1 = (bf16[128,256]{1,0:T(8,128)(2,1)S(1)}, bf16[128,256]{1,0:T(8,128)(2,1)S(1)}, u32[]{:S(2)}, u32[]{:S(2)}) collective-permute-start(bf16[128,256]{1,0:T(8,128)(2,1)S(1)} %collective-permute-done), channel_id=1, source_target_pairs={{0,4},{4,8},{8,12},{12,0},{1,5},{5,9},{9,13},{13,1},{2,6},{6,10},{... | collective-permute-start | bytes 196616 | tf_op jit(solution)/shard_map/ppermute | solution.py:31
  29.0 6.1 %collective-permute-start.2 = (bf16[128,256]{1,0:T(8,128)(2,1)S(1)}, bf16[128,256]{1,0:T(8,128)(2,1)S(1)}, u32[]{:S(2)}, u32[]{:S(2)}) collective-permute-start(bf16[128,256]{1,0:T(8,128)(2,1)S(1)} %collective-permute-done.1), channel_id=1, source_target_pairs={{0,4},{4,8},{8,12},{12,0},{1,5},{5,9},{9,13},{13,1},{2,6},{6,10},{... | collective-permute-start | bytes 196616 | tf_op jit(solution)/shard_map/ppermute | solution.py:31
  35.9 0.7 copy-start.1
  36.6 71.7 %reduce-scatter.5.cloned.1.call-start = ((), (), s32[]{:S(2)}) async-start(), calls=%async_computation.4 | async-start | bytes 1966080 | tf_op jit(solution)/shard_map/reduce_scatter | solution.py:77
Sparse Core Ops, SparseCore 0:
  12.8 34.1 reduce-scatter.2
  49.1 16.8 all-gather.1
  82.4 25.9 reduce-scatter.4
